TPU v7x, 512 devices: a whole 4x4x16 slice. The times are simulated.
512 devices in a mesh: ctx: 16 (over z), ch: 32 (over x, y, core).
Axes of the slice: x: 4, y: 4, z: 16, core: 2. Of those that a mesh axis runs over, the one named last changes fastest.
Arguments:
- features: bfloat16 [2, 16, 128, 3, 4096], P(None, 'ctx', None, None, 'ch'), may hold values from -6 to 6
- short_weight: bfloat16 [7, 3, 4096], P(None, None, 'ch'), may hold values from -2 to 2
- long_filter: bfloat16 [2, 16, 128, 4096], P(None, 'ctx', None, 'ch'), may hold values from -0.125 to 0.125
- skip_gain: float32 [4096], P('ch'), may hold values from -4 to 4
- out_weight: bfloat16 [4096, 4096], P('ch'), may hold values from -0.1875 to 0.1875
Outputs:
- mixed: bfloat16 [2, 16, 128, 4096], P(None, 'ctx', None, 'ch')
All inputs are finite; a program needn't handle non-finite values.
Results may differ from a plain program's by a relative error of at most 0.015.
Values may be sent and summed in bfloat16 or wider, within the bound.
No kernel may reach another device: no remote copies, remote signals or barrier semaphores. Data moves between devices by JAX's collectives and lax.ppermute only.
A program may use at most 64 MiB of HBM per device.

v0:
```python
import math
import jax
import jax.numpy as jnp
from jax import lax
from jax.sharding import PartitionSpec as P


def from_behind(value, axis, steps):
    count = lax.axis_size(axis)
    initial, last = (max(0, -steps), min(count, count - steps))
    return lax.ppermute(value, axis, [(source, source + steps) for source in range(initial, last)])


def transform_tables(length):
    period = 2 * length
    indices = jnp.arange(period, dtype=jnp.int32)
    phases = indices[:, None] * indices[None, :] % period
    angles = phases.astype(jnp.float32) * (2.0 * math.pi / period)
    cosine = jnp.cos(angles)
    sine_table = jnp.sin(angles)
    forward_full = jnp.concatenate([cosine, -sine_table], axis=0)
    forward_data = forward_full[:, :length]
    inverse = jnp.concatenate([cosine[:length], -sine_table[:length]], axis=1) / period
    return (forward_full, forward_data, inverse)


def complex_product(first, second):
    middle = first.shape[-2] // 2
    real_a = first[..., :middle, :]
    imag_a = first[..., middle:, :]
    real_b = second[..., :middle, :]
    imag_b = second[..., middle:, :]
    return jnp.concatenate(
        [real_a * real_b - imag_a * imag_b, real_a * imag_b + imag_a * real_b], axis=-2
    )


def featurize(tokens, before, kernel):
    extended = jnp.concatenate([before, tokens], axis=0).astype(jnp.float32)
    length = tokens.shape[0]
    margin_rows = kernel.shape[0] - 1
    summed = jnp.zeros(tokens.shape, jnp.float32)
    for offset in range(kernel.shape[0]):
        summed = (
            summed
            + kernel[offset].astype(jnp.float32)
            * extended[margin_rows - offset : margin_rows - offset + length]
        )
    return summed


def ordered(blocks):
    return jnp.concatenate([blocks[0], jnp.flip(blocks[1], axis=0)], axis=0)


def local(features, short_weight, long_filter, skip_gain, out_weight):
    pair_count = lax.axis_size("ctx")
    blocks_all = 2 * pair_count
    position = lax.axis_index("ctx")
    length = features.shape[2]
    margin_rows = short_weight.shape[0] - 1
    trailing = features[:, 0, length - margin_rows :]
    from_before = from_behind(trailing[0], "ctx", 1)
    from_after = from_behind(trailing[1], "ctx", -1)
    second_rim = jnp.where(position == pair_count - 1, trailing[0], from_after)
    first_feat = featurize(features[0, 0], from_before, short_weight)
    second_feat = featurize(features[1, 0], second_rim, short_weight)
    featured = jnp.stack([first_feat, second_feat], axis=0)
    queries = featured[:, :, 0]
    gated_keys = (featured[:, :, 1] * featured[:, :, 2]).astype(jnp.bfloat16)
    forward_full, forward_data, inverse = transform_tables(length)
    precise = lax.Precision.HIGHEST
    gathered = lax.all_gather(long_filter, "ctx", axis=1, tiled=True)
    lag_order = ordered(gathered)
    padded = jnp.concatenate(
        [jnp.zeros((1,) + lag_order.shape[1:], lag_order.dtype), lag_order], axis=0
    )
    lag_spectra = jnp.einsum(
        "fn,knc->kfc", forward_data, padded.astype(jnp.float32), precision=precise
    )
    frequency = jnp.arange(4 * length, dtype=jnp.int32) % (2 * length)
    parity = jnp.where(frequency % 2 == 0, 1.0, -1.0).astype(jnp.float32)[:, None]
    responses = lag_spectra[1:] + parity * lag_spectra[:-1]
    targets = jnp.stack([position, blocks_all - 1 - position])

    def absorb(totals, spectrum, source):
        for target_slot in range(2):
            distance = targets[target_slot] - source
            clamped = jnp.maximum(distance, 0)
            response = lax.dynamic_index_in_dim(responses, clamped, 0, keepdims=False)
            contribution = complex_product(response, spectrum)
            totals = totals.at[target_slot].add(jnp.where(distance >= 0, contribution, 0.0))
        return totals

    zeroed = jnp.zeros((2, 4 * length, gated_keys.shape[-1]), jnp.float32)

    def transform_block(values):
        return jnp.dot(forward_data, values.astype(jnp.float32), precision=precise)

    totals = zeroed
    shards = lax.all_gather(gated_keys[:, None], "ctx", axis=1, tiled=True)

    def advance(running, offset):
        couple = lax.dynamic_index_in_dim(shards, offset, 1, keepdims=False)
        running = absorb(running, transform_block(couple[0]), offset)
        running = absorb(running, transform_block(couple[1]), blocks_all - 1 - offset)
        return (running, None)

    totals, unused = lax.scan(advance, totals, jnp.arange(shards.shape[1], dtype=jnp.int32))
    convolved = jnp.einsum("tf,hfc->htc", inverse, totals, precision=precise)
    activated = (queries * (convolved + skip_gain * gated_keys.astype(jnp.float32))).astype(
        jnp.bfloat16
    )
    token_rows = activated.reshape(2 * length, activated.shape[-1])
    channels = token_rows.shape[1]
    owned = lax.psum_scatter(
        lax.dot_general(
            out_weight, token_rows, (((0,), (1,)), ((), ())), preferred_element_type=jnp.float32
        ).astype(jnp.bfloat16),
        "ch",
        scatter_dimension=0,
        tiled=True,
    ).astype(jnp.float32)
    result = owned.T
    return result.astype(jnp.bfloat16).reshape(2, 1, length, channels)


def solution(mesh):
    in_specs = (
        P(None, "ctx", None, None, "ch"),
        P(None, None, "ch"),
        P(None, "ctx", None, "ch"),
        P("ch"),
        P("ch", None),
    )
    out_specs = P(None, "ctx", None, "ch")
    return jax.shard_map(local, mesh=mesh, in_specs=in_specs, out_specs=out_specs, check_vma=False)
```

profile of v0, /device:TPU:2, one launch (start us, length us, event | category | flops | bytes accessed | tf_op | source)
XLA Modules:
  0.0 414.9 jit_solution(9419086972166073403)
XLA Ops:
  6.5 1.7 copy.15
  9.0 3.8 collective-permute-start
  12.8 1.3 collective-permute-start.1
  16.1 2.2 collective-permute-done.1
  22.3 62.3 %all-gather.4.cloned.1.call-done = bf16[2,16,128,128]{2,3,1,0:T(8,128)(2,1)} async-done(((bf16[2,1,128,128]{2,3,1,0:T(8,128)(2,1)}), bf16[2,16,128,128]{2,3,1,0:T(8,128)(2,1)}) %all-gather.4.cloned.1.call-update) | async-done | bytes 1048592 | tf_op jit(solution)/shard_map/all_gather | solution.py:73
  84.6 1.3 slice_bitcast_fusion.1
  85.9 3.7 convolution_bitcast_fusion.2
  89.6 4.5 %fusion.7 = f32[32,512,128]{1,2,0:T(8,128)} fusion(f32[33,512,128]{1,2,0:T(8,128)S(1)} %convolution_bitcast_fusion.2, f32[512]{0:T(512)S(1)} %fusion.56), kind=kLoop, calls=%fused_computation.35 | loop fusion | flops 4194304 | bytes 25167872 | tf_op jit(solution)/shard_map/add | solution.py:83
  94.2 60.3 %all-gather.6.cloned.1.call-done = bf16[2,2048,1,128]{3,1,0,2:T(8,128)(2,1)} async-done(((bf16[2,128,1,128]{3,1,0,2:T(8,128)(2,1)}), bf16[2,2048,1,128]{3,1,0,2:T(8,128)(2,1)}) %all-gather.6.cloned.1.call-update) | async-done | bytes 1048592 | tf_op jit(solution)/shard_map/all_gather | solution.py:101
  154.5 149.5 %while.16 = (s32[]{:T(128)}, f32[2,512,128]{1,2,0:T(8,128)S(1)}, s32[16]{0:T(128)S(1)}, s32[]{:T(128)}, f32[32,512,128]{1,2,0:T(8,128)}, /*index=5*/bf16[2,16,12...) while((s32[]{:T(128)}, f32[2,512,128]{1,2,0:T(8,128)S(1)}, ...), condition=%wide.region_1.2_spmd, body=%wide.region_0.1_spmd.sunk | while | flops 202899456 | bytes 6881675 | solution.py:109
  159.5 1.2 subtract_bitcast_fusion.6
  162.5 1.2 subtract_bitcast_fusion.7
  168.8 1.2 subtract_bitcast_fusion.6
  171.9 1.2 subtract_bitcast_fusion.7
  178.1 1.2 subtract_bitcast_fusion.6
  181.2 1.2 subtract_bitcast_fusion.7
  209.3 1.2 subtract_bitcast_fusion.7
  227.9 1.2 subtract_bitcast_fusion.7
  271.6 1.2 subtract_bitcast_fusion.6
  274.7 1.2 subtract_bitcast_fusion.7
  290.3 1.2 subtract_bitcast_fusion.6
  305.4 2.5 copy.19
  308.0 98.9 %reduce-scatter.4.cloned.1.call-done = bf16[128,256]{1,0:T(8,128)(2,1)} async-done(((bf16[4096,256]{1,0:T(8,128)(2,1)}), bf16[128,256]{1,0:T(8,128)(2,1)}) %reduce-scatter.4.cloned.1.call-update) | async-done | bytes 65552
  406.8 1.6 copy.20
  (171 shorter events, 80.7 us)
Async XLA Ops:
  6.5 298.2 %copy-start = (bf16[128,4096]{1,0:T(8,128)(2,1)S(1)}, bf16[128,4096]{1,0:T(8,128)(2,1)}, u32[]{:S(2)}) copy-start(bf16[128,4096]{1,0:T(8,128)(2,1)} %param.19) | copy-start | bytes 3145732
  6.5 78.1 %all-gather.4.cloned.1.call-start = ((), (), s32[]{:S(2)}) async-start(), calls=%async_computation.1 | async-start | bytes 1114112 | tf_op jit(solution)/shard_map/all_gather | solution.py:73
  8.2 146.2 %all-gather.6.cloned.1.call-start = ((), (), s32[]{:S(2)}) async-start(), calls=%async_computation.2 | async-start | bytes 1114112 | tf_op jit(solution)/shard_map/all_gather | solution.py:101
  9.0 10.1 %collective-permute-start = (bf16[6,3,128]{2,0,1:T(8,128)(2,1)S(1)}, bf16[6,3,128]{2,0,1:T(8,128)(2,1)S(1)}, u32[]{:S(2)}, u32[]{:S(2)}) collective-permute-start(bf16[6,3,128]{2,0,1:T(8,128)(2,1)S(1)} %get-tuple-element.184), channel_id=1, source_target_pairs={{0,32},{32,64},{64,96},{96,128},{128,160},{160,192},{192,224},{224... | collective-permute-start | bytes 13832 | tf_op jit(solution)/shard_map/ppermute | solution.py:11
  12.8 5.5 %collective-permute-start.1 = (bf16[6,3,128]{2,0,1:T(8,128)(2,1)S(1)}, bf16[6,3,128]{2,0,1:T(8,128)(2,1)S(1)}, u32[]{:S(2)}, u32[]{:S(2)}) collective-permute-start(bf16[6,3,128]{2,0,1:T(8,128)(2,1)S(1)} %get-tuple-element.183), channel_id=1, source_target_pairs={{32,0},{64,32},{96,64},{128,96},{160,128},{192,160},{224,192},{256... | collective-permute-start | bytes 13832 | tf_op jit(solution)/shard_map/ppermute | solution.py:11
  20.1 386.7 %reduce-scatter.4.cloned.1.call-start = ((), (), s32[]{:S(2)}) async-start(), calls=%async_computation.3 | async-start | bytes 2162688
  154.5 149.5 %copy-start.1 = (bf16[2,128,1,128]{3,1,0,2:T(8,128)(2,1)S(1)}, bf16[2,128,1,128]{3,1,0,2:T(8,128)(2,1)}, u32[]{:S(2)}) copy-start(bf16[2,128,1,128]{3,1,0,2:T(8,128)(2,1)} %fusion.44) | copy-start | bytes 196612
  154.5 149.5 %copy-start.2 = (f32[128]{0:T(128)S(1)}, f32[128]{0:T(128)}, u32[]{:S(2)}) copy-start(f32[128]{0:T(128)} %param.18) | copy-start | bytes 1540
Sparse Core Ops, SparseCore 0:
  9.4 75.1 all-gather.3
  86.7 67.7 all-gather.5
  308.1 98.7 reduce-scatter.3
where the time goes:
time: 419 us; the launch traced here: 415 us
  waiting for transfers between devices  224 us (53%)
  loops' own time  64 us (15%)
  other arithmetic  51 us (12%)
  matrix products  39.4 us (9%)
  local copies, waits for them, and re-layouts  18.2 us (4%)
  between operations  13.3 us (3%)
  starting transfers between devices  5.19 us (1%)
    unnamed x4, waiting for transfers between devices  98.9 us
    another operation x1, loops' own time, local(): lax.scan(advance, totals, jnp.arange(shards.shape[1], dtype=jnp.int32))  64 us
    all_gather x1, waiting for transfers between devices, local(): gathered = lax.all_gather(long_filter, 'ctx', axis=1, tiled=True)  62.3 us
    all_gather x1, waiting for transfers between devices, local(): shards = lax.all_gather(gated_keys[:, None], 'ctx', axis=1, tiled=True)  60.3 us
    concatenate x32, other arithmetic, complex_product(): jnp.concatenate([real_a * real_b - imag_a * imag_b, real_a * imag_b + ima...  37.2 us
    dot_general x32, matrix products, transform_block(): return jnp.dot(forward_data, values.astype(jnp.float32), precision=precise)  34.4 us
    dynamic_slice x16, local copies, waits for them, and re-layouts, local(): lax.scan(advance, totals, jnp.arange(shards.shape[1], dtype=jnp.int32))  9.38 us
  transfers between devices with their start and end apart: 5, of which 4 were waited for; matrix products, arithmetic and copies ran while one was open for 4% of the time, Pallas kernels for 0%

commit v1 on v0

--- a/solution.py
+++ b/solution.py
@@ -1,8 +1,24 @@
+import functools
 import math
 import jax
 import jax.numpy as jnp
 from jax import lax
 from jax.sharding import PartitionSpec as P
+
+
+def figure_assign(slab_in, on_dim):
+    return jnp.concatenate(
+        lax.all_to_all(
+            jnp.stack([slab_in for _ in range(lax.axis_size("ctx"))], 0),
+            axis_name="ctx",
+            split_axis=0,
+            concat_axis=0,
+        ),
+        on_dim,
+    )
+
+
+take_regions = functools.partial(figure_assign, on_dim=1)
 
 
 def from_behind(value, axis, steps):
@@ -98,7 +114,7 @@
         return jnp.dot(forward_data, values.astype(jnp.float32), precision=precise)
 
     totals = zeroed
-    shards = lax.all_gather(gated_keys[:, None], "ctx", axis=1, tiled=True)
+    shards = take_regions(gated_keys[:, None])
 
     def advance(running, offset):
         couple = lax.dynamic_index_in_dim(shards, offset, 1, keepdims=False)

time: 419 us -> 385 us (0.919)
  waiting for transfers between devices: 224 us -> 180 us
  matrix products: 39.4 us -> 16.4 us
  local copies, waits for them, and re-layouts: 18.2 us -> 34.6 us
  starting transfers between devices: 5.19 us -> 21.2 us
    all_gather x1 -> x0, waiting for transfers between devices: 60.3 us -> none  [local(): shards = lax.all_gather(gated_keys[:, None], 'ctx', axis=1, tiled=True)]
    dot_general x32, matrix products: 34.4 us -> 10.1 us  [transform_block(): return jnp.dot(forward_data, values.astype(jnp.float32), precision=precise)]
    all_gather x1, waiting for transfers between devices: 62.3 us -> 80.4 us  [local(): gathered = lax.all_gather(long_filter, 'ctx', axis=1, tiled=True)]
    all_to_all x0 -> x1, starting transfers between devices: none -> 15.2 us  [figure_assign(): lax.all_to_all(jnp.stack([slab_in for _ in range(lax.axis_size('ctx'))],...]
    dynamic_slice x0 -> x16, local copies, waits for them, and re-layouts: none -> 13.6 us  [advance(): couple = lax.dynamic_index_in_dim(shards, offset, 1, keepdims=False)]
    unnamed x4 -> x3, waiting for transfers between devices: 98.9 us -> 100 us
  transfers between devices with their start and end apart: 5 -> 5, of which waited for: 4 -> 2; matrix products, arithmetic and copies ran while one was open for 4% -> 5% of each run, Pallas kernels for 0% -> 0%
where the time goes in v1:
time: 385 us; the launch traced here: 382 us
  waiting for transfers between devices  180 us (47%)
  loops' own time  64 us (17%)
  other arithmetic  52 us (14%)
  local copies, waits for them, and re-layouts  34.6 us (9%)
  starting transfers between devices  21.2 us (6%)
  matrix products  16.4 us (4%)
  between operations  13.7 us (4%)
    unnamed x3, waiting for transfers between devices  100 us
    all_gather x1, waiting for transfers between devices, local(): gathered = lax.all_gather(long_filter, 'ctx', axis=1, tiled=True)  80.4 us
    another operation x1, loops' own time, local(): lax.scan(advance, totals, jnp.arange(shards.shape[1], dtype=jnp.int32))  64 us
    concatenate x32, other arithmetic, complex_product(): jnp.concatenate([real_a * real_b - imag_a * imag_b, real_a * imag_b + ima...  37.2 us
    all_to_all x1, starting transfers between devices, figure_assign(): lax.all_to_all(jnp.stack([slab_in for _ in range(lax.axis_size('ctx'))],...  15.2 us
    dynamic_slice x16, local copies, waits for them, and re-layouts, advance(): couple = lax.dynamic_index_in_dim(shards, offset, 1, keepdims=False)  13.6 us
    dot_general x32, matrix products, transform_block(): return jnp.dot(forward_data, values.astype(jnp.float32), precision=precise)  10.1 us
    dynamic_slice x16, local copies, waits for them, and re-layouts, local(): lax.scan(advance, totals, jnp.arange(shards.shape[1], dtype=jnp.int32))  9.38 us
  transfers between devices with their start and end apart: 5, of which 2 were waited for; matrix products, arithmetic and copies ran while one was open for 5% of the time, Pallas kernels for 0%

profile of v1, /device:TPU:2, one launch (start us, length us, event | category | flops | bytes accessed | tf_op | source)
XLA Modules:
  0.0 382.3 jit_solution(3466336878888789597)
XLA Ops:
  7.3 1.3 collective-permute-start.1
  8.6 4.5 %collective-permute-start = (bf16[6,3,128]{2,0,1:T(8,128)(2,1)S(1)}, bf16[6,3,128]{2,0,1:T(8,128)(2,1)S(1)}, u32[]{:S(2)}, u32[]{:S(2)}) collective-permute-start(bf16[6,3,128]{2,0,1:T(8,128)(2,1)S(1)} %get-tuple-element.191), channel_id=1, source_target_pairs={{0,32},{32,64},{64,96},{96,128},{128,160},{160,192},{192,224},{224... | collective-permute-start | bytes 13832 | tf_op jit(solution)/shard_map/ppermute | solution.py:27
  16.3 1.2 stack.15
  17.6 15.2 %all-to-all-start = ((bf16[16,2,1,128,128]{4,3,1,2,0:T(8,128)(2,1)}), bf16[16,2,1,128,128]{4,3,1,2,0:T(8,128)(2,1)}, u32[]{:S(2)}, u32[]{:S(2)}) async-start(bf16[16,2,1,128,128]{4,3,1,2,0:T(8,128)(2,1)} %stack.15), calls=%async_computation | async-start | bytes 2097152 | tf_op jit(solution)/shard_map/all_to_all | solution.py:11
  32.9 1.6 copy.15
  38.2 80.4 %all-gather.2.cloned.1.call-done = bf16[2,16,128,128]{2,3,1,0:T(8,128)(2,1)} async-done(((bf16[2,1,128,128]{2,3,1,0:T(8,128)(2,1)}), bf16[2,16,128,128]{2,3,1,0:T(8,128)(2,1)}) %all-gather.2.cloned.1.call-update) | async-done | bytes 1048592 | tf_op jit(solution)/shard_map/all_gather | solution.py:89
  118.6 1.3 slice_bitcast_fusion.5
  119.9 3.7 convolution_bitcast_fusion.2
  123.6 4.5 %fusion.5 = f32[32,512,128]{1,2,0:T(8,128)} fusion(f32[33,512,128]{1,2,0:T(8,128)S(1)} %convolution_bitcast_fusion.2, f32[512]{0:T(512)S(1)} %fusion.55), kind=kLoop, calls=%fused_computation.34 | loop fusion | flops 4194304 | bytes 25167872 | tf_op jit(solution)/shard_map/add | solution.py:99
  128.3 138.8 %while.16 = (s32[]{:T(128)}, f32[2,512,128]{1,2,0:T(8,128)S(1)}, s32[16]{0:T(128)S(1)}, s32[]{:T(128)}, f32[32,512,128]{1,2,0:T(8,128)}, /*index=5*/bf16[2,16,12...) while((s32[]{:T(128)}, f32[2,512,128]{1,2,0:T(8,128)S(1)}, ...), condition=%wide.region_1.2_spmd, body=%wide.region_0.1_spmd.sunk | while | flops 202899456 | bytes 7012719 | solution.py:125
  133.3 1.2 subtract_bitcast_fusion.6
  135.6 1.2 subtract_bitcast_fusion.7
  142.0 1.2 subtract_bitcast_fusion.6
  144.3 1.2 subtract_bitcast_fusion.7
  150.6 1.2 subtract_bitcast_fusion.6
  153.0 1.2 subtract_bitcast_fusion.7
  205.0 1.2 subtract_bitcast_fusion.7
  211.4 1.2 subtract_bitcast_fusion.6
  220.1 1.2 subtract_bitcast_fusion.6
  222.4 1.2 subtract_bitcast_fusion.7
  267.8 2.0 fusion.6
  269.8 4.1 %copy.20 = bf16[4096,256]{1,0:T(8,128)(2,1)} copy(bf16[4096,256]{0,1:T(8,128)(2,1)} %fusion.6) | data formatting | bytes 4194304
  273.9 100.0 %reduce-scatter.4.cloned.1.call-done = bf16[128,256]{1,0:T(8,128)(2,1)} async-done(((bf16[4096,256]{1,0:T(8,128)(2,1)}), bf16[128,256]{1,0:T(8,128)(2,1)}) %reduce-scatter.4.cloned.1.call-update) | async-done | bytes 65552
  373.9 1.6 copy.21
  (195 shorter events, 71.5 us)
Async XLA Ops:
  6.5 261.3 %copy-start = (bf16[128,4096]{1,0:T(8,128)(2,1)S(1)}, bf16[128,4096]{1,0:T(8,128)(2,1)}, u32[]{:S(2)}) copy-start(bf16[128,4096]{1,0:T(8,128)(2,1)} %param.19) | copy-start | bytes 3145732
  7.3 7.8 %collective-permute-start.1 = (bf16[6,3,128]{2,0,1:T(8,128)(2,1)S(1)}, bf16[6,3,128]{2,0,1:T(8,128)(2,1)S(1)}, u32[]{:S(2)}, u32[]{:S(2)}) collective-permute-start(bf16[6,3,128]{2,0,1:T(8,128)(2,1)S(1)} %get-tuple-element.192), channel_id=1, source_target_pairs={{32,0},{64,32},{96,64},{128,96},{160,128},{192,160},{224,192},{256... | collective-permute-start | bytes 13832 | tf_op jit(solution)/shard_map/ppermute | solution.py:27
  8.6 7.5 %collective-permute-start = (bf16[6,3,128]{2,0,1:T(8,128)(2,1)S(1)}, bf16[6,3,128]{2,0,1:T(8,128)(2,1)S(1)}, u32[]{:S(2)}, u32[]{:S(2)}) collective-permute-start(bf16[6,3,128]{2,0,1:T(8,128)(2,1)S(1)} %get-tuple-element.191), channel_id=1, source_target_pairs={{0,32},{32,64},{64,96},{96,128},{128,160},{160,192},{192,224},{224... | collective-permute-start | bytes 13832 | tf_op jit(solution)/shard_map/ppermute | solution.py:27
  16.3 20.2 %copy-start.2 = (bf16[2,128,128]{2,1,0:T(8,128)(2,1)}, bf16[2,128,128]{2,1,0:T(8,128)(2,1)S(1)}, u32[]{:S(2)}) copy-start(bf16[2,128,128]{2,1,0:T(8,128)(2,1)S(1)} %fusion.49) | copy-start | bytes 196612
  17.6 110.6 %all-to-all-start = ((bf16[16,2,1,128,128]{4,3,1,2,0:T(8,128)(2,1)}), bf16[16,2,1,128,128]{4,3,1,2,0:T(8,128)(2,1)}, u32[]{:S(2)}, u32[]{:S(2)}) async-start(bf16[16,2,1,128,128]{4,3,1,2,0:T(8,128)(2,1)} %stack.15), calls=%async_computation | async-start | bytes 2097152 | tf_op jit(solution)/shard_map/all_to_all | solution.py:11
  32.8 85.8 %all-gather.2.cloned.1.call-start = ((), (), s32[]{:S(2)}) async-start(), calls=%async_computation.2 | async-start | bytes 1114112 | tf_op jit(solution)/shard_map/all_gather | solution.py:89
  34.5 339.4 %reduce-scatter.4.cloned.1.call-start = ((), (), s32[]{:S(2)}) async-start(), calls=%async_computation.3 | async-start | bytes 2162688
  35.5 92.7 %copy-start.1 = (f32[256,256]{1,0:T(8,128)}, f32[256,256]{1,0:T(8,128)S(1)}, u32[]{:S(2)}) copy-start(f32[256,256]{1,0:T(8,128)S(1)} %fusion.47) | copy-start | bytes 786436
  128.2 138.9 %slice-start = ((f32[256,256]{1,0:T(8,128)}), f32[128,256]{1,0:T(8,128)S(1)}, s32[]{:S(2)}) async-start(f32[256,256]{1,0:T(8,128)} %copy-done.1), calls=%async_computation.4 | async-start | bytes 262144 | tf_op jit(solution)/shard_map/slice | solution.py:39
  128.2 138.9 %copy-start.3 = (bf16[2,128,128]{2,1,0:T(8,128)(2,1)S(1)}, bf16[2,128,128]{2,1,0:T(8,128)(2,1)}, u32[]{:S(2)}) copy-start(bf16[2,128,128]{2,1,0:T(8,128)(2,1)} %copy-done.2) | copy-start | bytes 196612
  128.3 138.9 %copy-start.4 = (f32[128,256]{1,0:T(8,128)S(1)}, f32[128,256]{1,0:T(8,128)}, u32[]{:S(2)}) copy-start(f32[128,256]{1,0:T(8,128)} %slice_negate_fusion) | copy-start | bytes 393220
  128.3 138.9 %copy-start.5 = (f32[128]{0:T(128)S(1)}, f32[128]{0:T(128)}, u32[]{:S(2)}) copy-start(f32[128]{0:T(128)} %param.18) | copy-start | bytes 1540
Sparse Core Ops, SparseCore 0:
  35.7 82.8 all-gather.1
  274.0 99.8 reduce-scatter.3
